TPU v7x, 32 devices: a whole 2x2x4 slice. The times are simulated.
32 devices in a mesh: grp: 2 (over x), row: 16 (over z, y, core).
Axes of the slice: x: 2, y: 2, z: 4, core: 2. Of those that a mesh axis runs over, the one named last changes fastest.
Arguments:
- node_feats: bfloat16 [512, 256], P(('grp', 'row')), parts along dimension 0, may hold values from -6 to 6
- pair_feats: bfloat16 [512, 256, 128], P(('grp', 'row')), parts along dimension 0, may hold values from -6 to 6
- trans: bfloat16 [512, 3], P(('grp', 'row')), parts along dimension 0, may hold values from -4 to 4
- frame_seed: int32 [512, 3], P(('grp', 'row')), parts along dimension 0, may hold values from 0 to 255
- residue_mask: int32 [512], P('grp'), parts along dimension 0, may hold values 0 or 1
- chain_index: int32 [512], P('grp'), parts along dimension 0, may hold values from 0 to 7, never falling along the last dimension, each value on 1 to 64 neighbouring positions
- w_qkv: bfloat16 [256, 576], replicated, may hold values from -0.375 to 0.375
- w_points: bfloat16 [256, 576], replicated, may hold values from -0.375 to 0.375
- w_bias: bfloat16 [128, 12], replicated, may hold values from -0.5 to 0.5
- head_weights: float32 [12], replicated, may hold values from -2 to 1
- chain_bias: float32 [12], replicated, may hold values from -6 to 6
- w_out: bfloat16 [2112, 256], replicated, may hold values from -0.125 to 0.125
- b_out: float32 [256], replicated, may hold values from -3 to 3
- w_trans: bfloat16 [3, 256, 256], replicated, may hold values from -0.375 to 0.375
- w_edge_node: bfloat16 [256, 128], replicated, may hold values from -0.375 to 0.375
- w_edge_in: bfloat16 [384, 384], replicated, may hold values from -0.3125 to 0.3125
- b_edge_in: float32 [384], replicated, may hold values from -3 to 3
- w_edge_mid: bfloat16 [384, 384], replicated, may hold values from -0.3125 to 0.3125
- b_edge_mid: float32 [384], replicated, may hold values from -3 to 3
- w_edge_out: bfloat16 [384, 128], replicated, may hold values from -0.3125 to 0.3125
- b_edge_out: float32 [128], replicated, may hold values from -3 to 3
Outputs:
- node_out: bfloat16 [512, 256], P(('grp', 'row')), parts along dimension 0
- pair_out: bfloat16 [512, 256, 128], P(('grp', 'row')), parts along dimension 0
There are 2 independent parts, one for each index of `grp`. A program takes and returns all parts, laid end to end along the dimension named above; an argument that names none is the same for every part. Nothing has to cross between parts.
Inputs may be any that keep to these rules, and one draw needn't show every extreme that they name: `chain_index`: never falls along the residues; a chain holds 1 to 64 residues.
All inputs are finite; a program needn't handle non-finite values.
Results may differ from a plain program's by a relative error of at most 0.013.
Values may be sent and summed in bfloat16 or wider, within the bound.
A program may use at most 64 MiB of HBM per device.

v0:
```python
import math

import jax
import jax.numpy as jnp
from jax import lax
from jax.sharding import PartitionSpec as P

C_PAIR = 128
HEADS = 12
HEAD_DIM = 16
QK_POINTS = 4
V_POINTS = 8
EDGE_NODE = 128


mask_bias = 100000.0
norm_eps = 1e-05
point_eps = 1e-08


def rotations(frame_seed):
    angles = frame_seed.astype(jnp.float32) * (2.0 * math.pi / 256.0)
    cosine = jnp.cos(angles)
    sine = jnp.sin(angles)
    zeros = jnp.zeros_like(cosine[:, 0])
    ones = jnp.ones_like(cosine[:, 0])

    def about_z(index):
        return jnp.stack(
            [
                jnp.stack([cosine[:, index], -sine[:, index], zeros], -1),
                jnp.stack([sine[:, index], cosine[:, index], zeros], -1),
                jnp.stack([zeros, zeros, ones], -1),
            ],
            -2,
        )

    about_y = jnp.stack(
        [
            jnp.stack([cosine[:, 1], zeros, sine[:, 1]], -1),
            jnp.stack([zeros, ones, zeros], -1),
            jnp.stack([-sine[:, 1], zeros, cosine[:, 1]], -1),
        ],
        -2,
    )
    return jnp.einsum(
        "nab,nbc,ncd->nad", about_z(0), about_y, about_z(2), precision=lax.Precision.HIGHEST
    )


def project_nodes(nodes, trans, rotate, w_plain, w_spatial):
    plain = jnp.dot(nodes, w_plain, preferred_element_type=jnp.float32).astype(jnp.bfloat16)
    local = jnp.dot(nodes, w_spatial, preferred_element_type=jnp.float32).reshape(
        nodes.shape[0], 3, -1
    )
    spatial = jnp.einsum("nab,nbk->nak", rotate, local, precision=lax.Precision.HIGHEST)
    spatial = spatial + trans.astype(jnp.float32)[:, :, None]
    return (plain, spatial.astype(jnp.bfloat16))


def layer_norm(values):
    centred = values - jnp.mean(values, -1, keepdims=True)
    return centred / jnp.sqrt(jnp.mean(centred * centred, -1, keepdims=True) + norm_eps)


def scores(
    query,
    qpoints,
    pair_block,
    key,
    kpoints,
    mask_q,
    mask_k,
    chain_q,
    chain_k,
    w_bias,
    head_weights,
    chain_bias,
):
    head_dim = query.shape[-1]
    qk_points = qpoints.shape[-1]
    dots = jnp.einsum("bhc,mhc->hbm", query, key, preferred_element_type=jnp.float32)
    bias = jnp.einsum("bmc,ch->hbm", pair_block, w_bias, preferred_element_type=jnp.float32)
    qfloat = qpoints.astype(jnp.float32)
    kfloat = kpoints.astype(jnp.float32)
    cross = jnp.einsum("bahp,mahp->hbm", qfloat, kfloat, precision=lax.Precision.HIGHEST)
    qsquare = jnp.sum(qfloat * qfloat, axis=(1, 3)).T
    ksquare = jnp.sum(kfloat * kfloat, axis=(1, 3)).T
    distance = qsquare[:, :, None] + ksquare[:, None, :] - 2.0 * cross
    gamma = jax.nn.softplus(head_weights)
    weight_c = math.sqrt(2.0 / (9.0 * qk_points))
    same = (chain_q[:, None] == chain_k[None, :]).astype(jnp.float32)
    pair_mask = (mask_q[:, None] * mask_k[None, :]).astype(jnp.float32)
    logit = math.sqrt(1.0 / 3.0) * (
        dots / math.sqrt(head_dim) + bias - 0.5 * weight_c * gamma[:, None, None] * distance
    )
    return logit + chain_bias[:, None, None] * same[None] + mask_bias * (pair_mask[None] - 1.0)


def update_nodes(
    nodes, node_part, point_part, pair_part, rotate, trans, mask_q, w_out, b_out, w_trans
):
    count = nodes.shape[0]
    shifted = point_part - trans.astype(jnp.float32)[:, :, None, None]
    local = jnp.einsum("bca,bchp->bahp", rotate, shifted, precision=lax.Precision.HIGHEST)
    length = jnp.sqrt(jnp.sum(local * local, 1) + point_eps)
    joined = jnp.concatenate(
        [
            node_part.reshape(count, -1),
            local.reshape(count, -1),
            length.reshape(count, -1),
            pair_part.reshape(count, -1),
        ],
        -1,
    ).astype(jnp.bfloat16)
    update = jnp.dot(joined, w_out, preferred_element_type=jnp.float32) + b_out
    first = layer_norm(nodes.astype(jnp.float32) + update).astype(jnp.bfloat16)
    hidden = jax.nn.relu(jnp.dot(first, w_trans[0], preferred_element_type=jnp.float32)).astype(
        jnp.bfloat16
    )
    hidden = jax.nn.relu(jnp.dot(hidden, w_trans[1], preferred_element_type=jnp.float32)).astype(
        jnp.bfloat16
    )
    last = jnp.dot(hidden, w_trans[2], preferred_element_type=jnp.float32)
    return (
        layer_norm(first.astype(jnp.float32) + last) * mask_q.astype(jnp.float32)[:, None]
    ).astype(jnp.bfloat16)


def key_parts(piece):
    width = HEADS * HEAD_DIM
    plain, spatial = piece
    count = plain.shape[0]
    spatial = spatial.reshape(count, 3, HEADS, QK_POINTS + V_POINTS)
    key = plain[:, :width].reshape(count, HEADS, HEAD_DIM)
    value = plain[:, width:].reshape(count, HEADS, HEAD_DIM)
    return (key, value, spatial[..., :QK_POINTS], spatial[..., QK_POINTS:])


def body(
    node_feats,
    pair_feats,
    trans,
    frame_seed,
    residue_mask,
    chain_index,
    w_qkv,
    w_points,
    w_bias,
    head_weights,
    chain_bias,
    w_out,
    b_out,
    w_trans,
    w_edge_node,
    w_edge_in,
    b_edge_in,
    w_edge_mid,
    b_edge_mid,
    w_edge_out,
    b_edge_out,
):
    rows = node_feats.shape[0]
    width = HEADS * HEAD_DIM
    offset = lax.axis_index("row") * rows
    mask_q = lax.dynamic_slice_in_dim(residue_mask, offset, rows)
    chain_q = lax.dynamic_slice_in_dim(chain_index, offset, rows)
    rotate = rotations(frame_seed)
    plain, spatial = project_nodes(node_feats, trans, rotate, w_qkv, w_points)
    spatial = spatial.reshape(rows, 3, HEADS, 2 * QK_POINTS + V_POINTS)
    query = plain[:, :width].reshape(rows, HEADS, HEAD_DIM)
    qpoints = spatial[..., :QK_POINTS]
    projected = (plain[:, width:], spatial[..., QK_POINTS:].reshape(rows, -1))
    whole = (
        lax.all_gather(projected[0], "row", axis=0, tiled=True),
        lax.all_gather(projected[1], "row", axis=0, tiled=True),
    )
    key, value, kpoints, vpoints = key_parts(whole)
    count = key.shape[0]
    pair_block = pair_feats
    mask_k = residue_mask
    logit = scores(
        query,
        qpoints,
        pair_block,
        key,
        kpoints,
        mask_q,
        mask_k,
        chain_q,
        chain_index,
        w_bias,
        head_weights,
        chain_bias,
    )
    logit, value, vpoints, pair_block = (logit, value, vpoints, pair_block)
    expo = jnp.exp(logit - jnp.max(logit, 2, keepdims=True))
    total = jnp.sum(expo, 2)
    weights = expo.astype(jnp.bfloat16)
    node_part = jnp.einsum("hbm,mhc->bhc", weights, value, preferred_element_type=jnp.float32)
    point_part = jnp.einsum("hbm,mahp->bahp", weights, vpoints, preferred_element_type=jnp.float32)
    pair_part = jnp.einsum("hbm,bmc->bhc", weights, pair_block, preferred_element_type=jnp.float32)
    total, parts = (total, (node_part, point_part, pair_part))
    totals = total.T
    node_part = parts[0] / totals[:, :, None]
    point_part = parts[1] / totals[:, None, :, None]
    pair_part = parts[2] / totals[:, :, None]
    node_out = update_nodes(
        node_feats, node_part, point_part, pair_part, rotate, trans, mask_q, w_out, b_out, w_trans
    )
    endpoint = jnp.dot(node_out, w_edge_node, preferred_element_type=jnp.float32).astype(
        jnp.bfloat16
    )
    near = (
        jnp.dot(
            endpoint, w_edge_in[C_PAIR : C_PAIR + EDGE_NODE], preferred_element_type=jnp.float32
        )
        + b_edge_in
    )
    mask_rows = mask_q.astype(jnp.float32)
    piece = lax.all_gather(endpoint, "row", axis=0, tiled=True)
    count = piece.shape[0]
    pair_block = pair_feats
    mask_k = residue_mask.astype(jnp.float32)
    far = jnp.dot(piece, w_edge_in[C_PAIR + EDGE_NODE :], preferred_element_type=jnp.float32)

    def one_row(inputs):
        pair_row, near_row, own_row, mask_row = inputs
        pre = (
            jnp.dot(pair_row, w_edge_in[:C_PAIR], preferred_element_type=jnp.float32)
            + near_row[None, :]
            + far
        )
        first = jax.nn.relu(pre).astype(jnp.bfloat16)
        second = jax.nn.relu(
            jnp.dot(first, w_edge_mid, preferred_element_type=jnp.float32) + b_edge_mid
        )
        joined = jnp.concatenate(
            [pair_row, jnp.broadcast_to(own_row[None, :], (count, EDGE_NODE)), piece], -1
        )
        resid = (second + joined.astype(jnp.float32)).astype(jnp.bfloat16)
        out = jnp.dot(resid, w_edge_out, preferred_element_type=jnp.float32) + b_edge_out
        return (layer_norm(out) * (mask_row * mask_k)[:, None]).astype(jnp.bfloat16)

    pair_out = lax.map(one_row, (pair_block, near, endpoint, mask_rows))
    return (node_out, pair_out)


def solution(mesh):
    in_specs = (
        P(("grp", "row"), None),
        P(("grp", "row"), None, None),
        P(("grp", "row"), None),
        P(("grp", "row"), None),
        P("grp"),
        P("grp"),
        P(),
        P(),
        P(),
        P(),
        P(),
        P(),
        P(),
        P(),
        P(),
        P(),
        P(),
        P(),
        P(),
        P(),
        P(),
    )
    out_specs = (P(("grp", "row"), None), P(("grp", "row"), None, None))
    return jax.shard_map(body, mesh=mesh, in_specs=in_specs, out_specs=out_specs, check_vma=False)
```

profile of v0, /device:TPU:0, one launch (start us, length us, event | category | flops | bytes accessed | tf_op | source)
XLA Modules:
  0.0 137.9 jit_solution(7205860032383303762)
XLA Ops:
  0.6 0.8 fusion.62
  3.7 1.2 fusion.75
  5.0 0.8 copy.123
  6.6 24.0 %all_gather.10 = bf16[256,432]{1,0:T(8,128)(2,1)S(1)} all-gather(bf16[16,432]{1,0:T(8,128)(2,1)S(1)} %reshape.162), channel_id=1, replica_groups=mesh['grp'=2,'row'=16] {'row'}, dimensions={0}, use_global_device_ids=true | all-gather | bytes 235008 | tf_op jit(solution)/shard_map/all_gather | solution.py:176
  32.1 18.0 %all_gather.9 = bf16[256,384]{1,0:T(8,128)(2,1)S(1)} all-gather(bf16[16,384]{1,0:T(8,128)(2,1)S(1)} %slice.85), channel_id=1, replica_groups=mesh['grp'=2,'row'=16] {'row'}, dimensions={0}, use_global_device_ids=true | all-gather | bytes 208896 | tf_op jit(solution)/shard_map/all_gather | solution.py:175
  52.3 0.9 multiply_reduce_fusion.1
  55.9 18.9 %all_gather.11 = bf16[256,128]{1,0:T(8,128)(2,1)S(1)} all-gather(bf16[16,128]{1,0:T(8,128)(2,1)S(1)} %convolution_convert_fusion.1), channel_id=1, replica_groups=mesh['grp'=2,'row'=16] {'row'}, dimensions={0}, use_global_device_ids=true | all-gather | bytes 69632 | tf_op jit(solution)/shard_map/all_gather | solution.py:221
  75.2 62.7 %while.10 = (s32[]{:T(128)}, bf16[16,256,128]{2,1,0:T(8,128)(2,1)}, bf16[16,256,128]{2,1,0:T(8,128)(2,1)S(1)}, bf16[384,384]{1,0:T(8,128)(2,1)S(1)}, f32[16,384]...) while((s32[]{:T(128)}, bf16[16,256,128]{2,1,0:T(8,128)(2,1)}, ...), condition=%wide.region_12.13_spmd, body=%wide.region_9.12_spmd.sunk | while | flops 127500800 | bytes 2349747 | solution.py:245
  75.3 1.4 %fusion.122 = bf16[256,384]{1,0:T(8,128)(2,1)S(1)} fusion(bf16[384,384]{1,0:T(8,128)(2,1)} %get-tuple-element.289, f32[256,384]{1,0:T(8,128)S(1)} %get-tuple-element.288, bf16[256,128]{1,0:T(8,128)(2,1)S(1)} %dynamic-slice_bitcast_fusion.2, bf16[256,128]{1,0:T(8,128)(2,1)S(1)} %get-tuple-element.292, f32[384]{0:T(512)S(1)} %get-tuple-element.290, ...), kind=kOutput, calls=%fused_computation.7.clone.1 | convolution fusion | flops 102039552 | bytes 1184768 | tf_op jit(solution)/shard_map/while/body/eval_jaxpr/dot_general | solution.py:236
  77.6 0.7 add_sqrt_fusion.4
  79.2 1.4 %fusion.122 = bf16[256,384]{1,0:T(8,128)(2,1)S(1)} fusion(bf16[384,384]{1,0:T(8,128)(2,1)} %get-tuple-element.289, f32[256,384]{1,0:T(8,128)S(1)} %get-tuple-element.288, bf16[256,128]{1,0:T(8,128)(2,1)S(1)} %dynamic-slice_bitcast_fusion.2, bf16[256,128]{1,0:T(8,128)(2,1)S(1)} %get-tuple-element.292, f32[384]{0:T(512)S(1)} %get-tuple-element.290, ...), kind=kOutput, calls=%fused_computation.7.clone.1 | convolution fusion | flops 102039552 | bytes 1184768 | tf_op jit(solution)/shard_map/while/body/eval_jaxpr/dot_general | solution.py:236
  81.6 0.7 add_sqrt_fusion.4
  83.1 1.4 %fusion.122 = bf16[256,384]{1,0:T(8,128)(2,1)S(1)} fusion(bf16[384,384]{1,0:T(8,128)(2,1)} %get-tuple-element.289, f32[256,384]{1,0:T(8,128)S(1)} %get-tuple-element.288, bf16[256,128]{1,0:T(8,128)(2,1)S(1)} %dynamic-slice_bitcast_fusion.2, bf16[256,128]{1,0:T(8,128)(2,1)S(1)} %get-tuple-element.292, f32[384]{0:T(512)S(1)} %get-tuple-element.290, ...), kind=kOutput, calls=%fused_computation.7.clone.1 | convolution fusion | flops 102039552 | bytes 1184768 | tf_op jit(solution)/shard_map/while/body/eval_jaxpr/dot_general | solution.py:236
  85.5 0.7 add_sqrt_fusion.4
  87.0 1.4 %fusion.122 = bf16[256,384]{1,0:T(8,128)(2,1)S(1)} fusion(bf16[384,384]{1,0:T(8,128)(2,1)} %get-tuple-element.289, f32[256,384]{1,0:T(8,128)S(1)} %get-tuple-element.288, bf16[256,128]{1,0:T(8,128)(2,1)S(1)} %dynamic-slice_bitcast_fusion.2, bf16[256,128]{1,0:T(8,128)(2,1)S(1)} %get-tuple-element.292, f32[384]{0:T(512)S(1)} %get-tuple-element.290, ...), kind=kOutput, calls=%fused_computation.7.clone.1 | convolution fusion | flops 102039552 | bytes 1184768 | tf_op jit(solution)/shard_map/while/body/eval_jaxpr/dot_general | solution.py:236
  89.4 0.7 add_sqrt_fusion.4
  90.9 1.4 %fusion.122 = bf16[256,384]{1,0:T(8,128)(2,1)S(1)} fusion(bf16[384,384]{1,0:T(8,128)(2,1)} %get-tuple-element.289, f32[256,384]{1,0:T(8,128)S(1)} %get-tuple-element.288, bf16[256,128]{1,0:T(8,128)(2,1)S(1)} %dynamic-slice_bitcast_fusion.2, bf16[256,128]{1,0:T(8,128)(2,1)S(1)} %get-tuple-element.292, f32[384]{0:T(512)S(1)} %get-tuple-element.290, ...), kind=kOutput, calls=%fused_computation.7.clone.1 | convolution fusion | flops 102039552 | bytes 1184768 | tf_op jit(solution)/shard_map/while/body/eval_jaxpr/dot_general | solution.py:236
  93.3 0.7 add_sqrt_fusion.4
  94.9 1.4 %fusion.122 = bf16[256,384]{1,0:T(8,128)(2,1)S(1)} fusion(bf16[384,384]{1,0:T(8,128)(2,1)} %get-tuple-element.289, f32[256,384]{1,0:T(8,128)S(1)} %get-tuple-element.288, bf16[256,128]{1,0:T(8,128)(2,1)S(1)} %dynamic-slice_bitcast_fusion.2, bf16[256,128]{1,0:T(8,128)(2,1)S(1)} %get-tuple-element.292, f32[384]{0:T(512)S(1)} %get-tuple-element.290, ...), kind=kOutput, calls=%fused_computation.7.clone.1 | convolution fusion | flops 102039552 | bytes 1184768 | tf_op jit(solution)/shard_map/while/body/eval_jaxpr/dot_general | solution.py:236
  97.2 0.7 add_sqrt_fusion.4
  98.8 1.4 %fusion.122 = bf16[256,384]{1,0:T(8,128)(2,1)S(1)} fusion(bf16[384,384]{1,0:T(8,128)(2,1)} %get-tuple-element.289, f32[256,384]{1,0:T(8,128)S(1)} %get-tuple-element.288, bf16[256,128]{1,0:T(8,128)(2,1)S(1)} %dynamic-slice_bitcast_fusion.2, bf16[256,128]{1,0:T(8,128)(2,1)S(1)} %get-tuple-element.292, f32[384]{0:T(512)S(1)} %get-tuple-element.290, ...), kind=kOutput, calls=%fused_computation.7.clone.1 | convolution fusion | flops 102039552 | bytes 1184768 | tf_op jit(solution)/shard_map/while/body/eval_jaxpr/dot_general | solution.py:236
  101.1 0.7 add_sqrt_fusion.4
  102.7 1.4 %fusion.122 = bf16[256,384]{1,0:T(8,128)(2,1)S(1)} fusion(bf16[384,384]{1,0:T(8,128)(2,1)} %get-tuple-element.289, f32[256,384]{1,0:T(8,128)S(1)} %get-tuple-element.288, bf16[256,128]{1,0:T(8,128)(2,1)S(1)} %dynamic-slice_bitcast_fusion.2, bf16[256,128]{1,0:T(8,128)(2,1)S(1)} %get-tuple-element.292, f32[384]{0:T(512)S(1)} %get-tuple-element.290, ...), kind=kOutput, calls=%fused_computation.7.clone.1 | convolution fusion | flops 102039552 | bytes 1184768 | tf_op jit(solution)/shard_map/while/body/eval_jaxpr/dot_general | solution.py:236
  105.1 0.7 add_sqrt_fusion.4
  106.6 1.4 %fusion.122 = bf16[256,384]{1,0:T(8,128)(2,1)S(1)} fusion(bf16[384,384]{1,0:T(8,128)(2,1)} %get-tuple-element.289, f32[256,384]{1,0:T(8,128)S(1)} %get-tuple-element.288, bf16[256,128]{1,0:T(8,128)(2,1)S(1)} %dynamic-slice_bitcast_fusion.2, bf16[256,128]{1,0:T(8,128)(2,1)S(1)} %get-tuple-element.292, f32[384]{0:T(512)S(1)} %get-tuple-element.290, ...), kind=kOutput, calls=%fused_computation.7.clone.1 | convolution fusion | flops 102039552 | bytes 1184768 | tf_op jit(solution)/shard_map/while/body/eval_jaxpr/dot_general | solution.py:236
  110.5 1.4 %fusion.122 = bf16[256,384]{1,0:T(8,128)(2,1)S(1)} fusion(bf16[384,384]{1,0:T(8,128)(2,1)} %get-tuple-element.289, f32[256,384]{1,0:T(8,128)S(1)} %get-tuple-element.288, bf16[256,128]{1,0:T(8,128)(2,1)S(1)} %dynamic-slice_bitcast_fusion.2, bf16[256,128]{1,0:T(8,128)(2,1)S(1)} %get-tuple-element.292, f32[384]{0:T(512)S(1)} %get-tuple-element.290, ...), kind=kOutput, calls=%fused_computation.7.clone.1 | convolution fusion | flops 102039552 | bytes 1184768 | tf_op jit(solution)/shard_map/while/body/eval_jaxpr/dot_general | solution.py:236
  114.4 1.4 %fusion.122 = bf16[256,384]{1,0:T(8,128)(2,1)S(1)} fusion(bf16[384,384]{1,0:T(8,128)(2,1)} %get-tuple-element.289, f32[256,384]{1,0:T(8,128)S(1)} %get-tuple-element.288, bf16[256,128]{1,0:T(8,128)(2,1)S(1)} %dynamic-slice_bitcast_fusion.2, bf16[256,128]{1,0:T(8,128)(2,1)S(1)} %get-tuple-element.292, f32[384]{0:T(512)S(1)} %get-tuple-element.290, ...), kind=kOutput, calls=%fused_computation.7.clone.1 | convolution fusion | flops 102039552 | bytes 1184768 | tf_op jit(solution)/shard_map/while/body/eval_jaxpr/dot_general | solution.py:236
  118.4 1.4 %fusion.122 = bf16[256,384]{1,0:T(8,128)(2,1)S(1)} fusion(bf16[384,384]{1,0:T(8,128)(2,1)} %get-tuple-element.289, f32[256,384]{1,0:T(8,128)S(1)} %get-tuple-element.288, bf16[256,128]{1,0:T(8,128)(2,1)S(1)} %dynamic-slice_bitcast_fusion.2, bf16[256,128]{1,0:T(8,128)(2,1)S(1)} %get-tuple-element.292, f32[384]{0:T(512)S(1)} %get-tuple-element.290, ...), kind=kOutput, calls=%fused_computation.7.clone.1 | convolution fusion | flops 102039552 | bytes 1184768 | tf_op jit(solution)/shard_map/while/body/eval_jaxpr/dot_general | solution.py:236
  122.3 1.4 %fusion.122 = bf16[256,384]{1,0:T(8,128)(2,1)S(1)} fusion(bf16[384,384]{1,0:T(8,128)(2,1)} %get-tuple-element.289, f32[256,384]{1,0:T(8,128)S(1)} %get-tuple-element.288, bf16[256,128]{1,0:T(8,128)(2,1)S(1)} %dynamic-slice_bitcast_fusion.2, bf16[256,128]{1,0:T(8,128)(2,1)S(1)} %get-tuple-element.292, f32[384]{0:T(512)S(1)} %get-tuple-element.290, ...), kind=kOutput, calls=%fused_computation.7.clone.1 | convolution fusion | flops 102039552 | bytes 1184768 | tf_op jit(solution)/shard_map/while/body/eval_jaxpr/dot_general | solution.py:236
  126.2 1.4 %fusion.122 = bf16[256,384]{1,0:T(8,128)(2,1)S(1)} fusion(bf16[384,384]{1,0:T(8,128)(2,1)} %get-tuple-element.289, f32[256,384]{1,0:T(8,128)S(1)} %get-tuple-element.288, bf16[256,128]{1,0:T(8,128)(2,1)S(1)} %dynamic-slice_bitcast_fusion.2, bf16[256,128]{1,0:T(8,128)(2,1)S(1)} %get-tuple-element.292, f32[384]{0:T(512)S(1)} %get-tuple-element.290, ...), kind=kOutput, calls=%fused_computation.7.clone.1 | convolution fusion | flops 102039552 | bytes 1184768 | tf_op jit(solution)/shard_map/while/body/eval_jaxpr/dot_general | solution.py:236
  130.1 1.4 %fusion.122 = bf16[256,384]{1,0:T(8,128)(2,1)S(1)} fusion(bf16[384,384]{1,0:T(8,128)(2,1)} %get-tuple-element.289, f32[256,384]{1,0:T(8,128)S(1)} %get-tuple-element.288, bf16[256,128]{1,0:T(8,128)(2,1)S(1)} %dynamic-slice_bitcast_fusion.2, bf16[256,128]{1,0:T(8,128)(2,1)S(1)} %get-tuple-element.292, f32[384]{0:T(512)S(1)} %get-tuple-element.290, ...), kind=kOutput, calls=%fused_computation.7.clone.1 | convolution fusion | flops 102039552 | bytes 1184768 | tf_op jit(solution)/shard_map/while/body/eval_jaxpr/dot_general | solution.py:236
  134.0 1.4 %fusion.122 = bf16[256,384]{1,0:T(8,128)(2,1)S(1)} fusion(bf16[384,384]{1,0:T(8,128)(2,1)} %get-tuple-element.289, f32[256,384]{1,0:T(8,128)S(1)} %get-tuple-element.288, bf16[256,128]{1,0:T(8,128)(2,1)S(1)} %dynamic-slice_bitcast_fusion.2, bf16[256,128]{1,0:T(8,128)(2,1)S(1)} %get-tuple-element.292, f32[384]{0:T(512)S(1)} %get-tuple-element.290, ...), kind=kOutput, calls=%fused_computation.7.clone.1 | convolution fusion | flops 102039552 | bytes 1184768 | tf_op jit(solution)/shard_map/while/body/eval_jaxpr/dot_general | solution.py:236
  (289 shorter events, 43.6 us)
Async XLA Ops:
  0.6 53.6 %copy-start = (bf16[2112,256]{1,0:T(8,128)(2,1)S(1)}, bf16[2112,256]{1,0:T(8,128)(2,1)}, u32[]{:S(2)}) copy-start(bf16[2112,256]{1,0:T(8,128)(2,1)} %param.34) | copy-start | bytes 3244036
  6.3 24.9 %copy-start.18 = (f32[12]{0:T(128)S(1)}, f32[12]{0:T(128)}, u32[]{:S(2)}) copy-start(f32[12]{0:T(128)} %param.32) | copy-start | bytes 148
  6.6 24.9 %copy-start.9 = (s32[256]{0:T(256)S(1)}, s32[256]{0:T(256)}, u32[]{:S(2)}) copy-start(s32[256]{0:T(256)} %param.27) | copy-start | bytes 3076
  6.6 25.1 %copy-start.14 = (s32[256]{0:T(256)S(1)}, s32[256]{0:T(256)}, u32[]{:S(2)}) copy-start(s32[256]{0:T(256)} %param.28) | copy-start | bytes 3076
  6.6 25.2 %copy-start.3 = (bf16[256,576]{0,1:T(8,128)(2,1)S(1)}, bf16[256,576]{0,1:T(8,128)(2,1)}, u32[]{:S(2)}) copy-start(bf16[256,576]{0,1:T(8,128)(2,1)} %param.29) | copy-start | bytes 884740
  6.6 25.2 %copy-start.5 = (bf16[16,256]{1,0:T(8,128)(2,1)S(1)}, bf16[16,256]{1,0:T(8,128)(2,1)}, u32[]{:S(2)}) copy-start(bf16[16,256]{1,0:T(8,128)(2,1)} %param.23) | copy-start | bytes 24580
  31.2 19.2 %copy-start.1 = (bf16[16,256,128]{2,1,0:T(8,128)(2,1)S(1)}, bf16[16,256,128]{2,1,0:T(8,128)(2,1)}, u32[]{:S(2)}) copy-start(bf16[16,256,128]{2,1,0:T(8,128)(2,1)} %param.24) | copy-start | bytes 3145732
  31.2 19.2 %copy-start.10 = (bf16[128,12]{0,1:T(8,128)(2,1)S(1)}, bf16[128,12]{0,1:T(8,128)(2,1)}, u32[]{:S(2)}) copy-start(bf16[128,12]{0,1:T(8,128)(2,1)} %param.31) | copy-start | bytes 9220
  50.1 0.7 copy-start.15
  50.8 0.9 copy-start.11
  52.2 2.0 %copy-start.13 = (f32[256]{0:T(256)S(1)}, f32[256]{0:T(256)}, u32[]{:S(2)}) copy-start(f32[256]{0:T(256)} %param.35) | copy-start | bytes 3076
  53.7 1.1 copy-start.16
  54.0 1.7 %copy-start.6 = (bf16[256,128]{1,0:T(8,128)(2,1)S(1)}, bf16[256,128]{1,0:T(8,128)(2,1)}, u32[]{:S(2)}) copy-start(bf16[256,128]{1,0:T(8,128)(2,1)} %param.37) | copy-start | bytes 196612
  54.1 20.8 %copy-start.4 = (bf16[384,384]{1,0:T(8,128)(2,1)S(1)}, bf16[384,384]{1,0:T(8,128)(2,1)}, u32[]{:S(2)}) copy-start(bf16[384,384]{1,0:T(8,128)(2,1)} %param.38) | copy-start | bytes 884740
  54.2 20.8 %copy-start.12 = (f32[384]{0:T(512)S(1)}, f32[384]{0:T(512)}, u32[]{:S(2)}) copy-start(f32[384]{0:T(512)} %param.39) | copy-start | bytes 4612
  54.2 20.9 %copy-start.2 = (bf16[384,128]{1,0:T(8,128)(2,1)S(1)}, bf16[384,128]{1,0:T(8,128)(2,1)}, u32[]{:S(2)}) copy-start(bf16[384,128]{1,0:T(8,128)(2,1)} %param.42) | copy-start | bytes 294916
  54.2 20.9 %copy-start.8 = (f32[128]{0:T(128)S(1)}, f32[128]{0:T(128)}, u32[]{:S(2)}) copy-start(f32[128]{0:T(128)} %param.43) | copy-start | bytes 1540
  54.2 20.9 %copy-start.17 = (f32[384]{0:T(512)S(1)}, f32[384]{0:T(512)}, u32[]{:S(2)}) copy-start(f32[384]{0:T(512)} %param.41) | copy-start | bytes 4612
  55.7 19.4 %copy-start.7 = (bf16[16,256]{1,0:T(8,128)(2,1)}, bf16[16,256]{1,0:T(8,128)(2,1)S(1)}, u32[]{:S(2)}) copy-start(bf16[16,256]{1,0:T(8,128)(2,1)S(1)} %multiply_convert_fusion.1) | copy-start | bytes 24580
where the time goes:
time: 139 us; the launch traced here: 138 us
  blocking collectives  60.9 us (44%)
  matrix products  32 us (23%)
  local copies, waits for them, and re-layouts  27.6 us (20%)
  other arithmetic  15.4 us (11%)
    all_gather x1, blocking collectives, body(): lax.all_gather(projected[1], 'row', axis=0, tiled=True)  24 us
    dot_general x16, matrix products, one_row(): jnp.dot(first, w_edge_mid, preferred_element_type=jnp.float32) + b_edge_mid  22.2 us
    all_gather x1, blocking collectives, body(): piece = lax.all_gather(endpoint, 'row', axis=0, tiled=True)  18.9 us
    all_gather x1, blocking collectives, body(): lax.all_gather(projected[0], 'row', axis=0, tiled=True)  18 us
    dynamic_update_slice x32, local copies, waits for them, and re-layouts, body(): pair_out = lax.map(one_row, (pair_block, near, endpoint, mask_rows))  12 us
    sqrt x18, other arithmetic, layer_norm(): jnp.sqrt(jnp.mean(centred * centred, -1, keepdims=True) + norm_eps)  11.1 us
    dynamic_slice x32, local copies, waits for them, and re-layouts, body(): pair_out = lax.map(one_row, (pair_block, near, endpoint, mask_rows))  11.1 us
    dot_general x16, matrix products, one_row(): jnp.dot(resid, w_edge_out, preferred_element_type=jnp.float32) + b_edge_out  3.96 us

commit v1 on v0

v1 whole, which is shorter than its diff:
```python
import functools
import math

import jax
import jax.numpy as jnp
from jax import lax
from jax.experimental import pallas as pl
from jax.experimental.pallas import tpu as pltpu
from jax.sharding import PartitionSpec as P

C_PAIR = 128
HEADS = 12
HEAD_DIM = 16
QK_POINTS = 4
V_POINTS = 8
POINTS = 2 * QK_POINTS + V_POINTS
EDGE_NODE = 128
WIDTH = HEADS * HEAD_DIM
PACK = 16
FRAME = 128

mask_bias = 100000.0
norm_eps = 1e-05
point_eps = 1e-08
F32 = jnp.float32
BF16 = jnp.bfloat16
MESH = pl.DeviceIdType.MESH
VMEM_LIMIT = 60 << 20


def dot(a, b):
    return jnp.dot(a, b, preferred_element_type=F32)


def dot_nt(a, b):
    return lax.dot_general(a, b, (((1,), (1,)), ((), ())), preferred_element_type=F32)


def layer_norm(values):
    centred = values - jnp.mean(values, -1, keepdims=True)
    return centred * lax.rsqrt(jnp.mean(centred * centred, -1, keepdims=True) + norm_eps)


def cos_sin(steps):
    quarter = jnp.floor((steps + 32.0) * (1.0 / 64.0))
    x = (steps - 64.0 * quarter) * (2.0 * math.pi / 256.0)
    y = x * x
    c = 1.0 + y * (-0.5 + y * (1 / 24 + y * (-1 / 720 + y * (1 / 40320 - y * (1 / 3628800)))))
    s = x * (1.0 + y * (-1 / 6 + y * (1 / 120 + y * (-1 / 5040 + y * (1 / 362880)))))
    one, two, three = quarter == 1.0, quarter == 2.0, quarter == 3.0
    cosine = jnp.where(one, -s, jnp.where(two, -c, jnp.where(three, s, c)))
    sine = jnp.where(one, c, jnp.where(two, -s, jnp.where(three, -c, s)))
    return cosine, sine


def frames(frame):
    cosine, sine = cos_sin(frame)
    c0, c1, c2 = (cosine[:, k : k + 1] for k in (3, 4, 5))
    s0, s1, s2 = (sine[:, k : k + 1] for k in (3, 4, 5))
    rotate = (
        (c0 * c1 * c2 - s0 * s2, -c0 * c1 * s2 - s0 * c2, c0 * s1),
        (s0 * c1 * c2 + c0 * s2, c0 * c2 - s0 * c1 * s2, s0 * s1),
        (-s1 * c2, s1 * s2, c1),
    )
    return rotate, tuple(frame[:, k : k + 1] for k in range(3))


def spatial_points(nodes, rotate, trans, w_points):
    local = [dot(nodes, w_points[:, b * WIDTH : (b + 1) * WIDTH]) for b in range(3)]
    return [
        (
            rotate[a][0] * local[0] + rotate[a][1] * local[1] + rotate[a][2] * local[2] + trans[a]
        ).astype(BF16)
        for a in range(3)
    ]


def iota(shape, axis):
    return lax.broadcasted_iota(jnp.int32, shape, axis)


def node_kernel(
    n,
    packed,
    mask_ref,
    chain_ref,
    w_bias,
    head_weights,
    chain_bias,
    b_out,
    w_edge_node,
    pair_hbm,
    w_qkv_hbm,
    w_points_hbm,
    w_out_hbm,
    w_trans_hbm,
    node_out,
    ends_out,
    own_out,
    gathered,
    ends,
    own_end,
    pair,
    w_qkv,
    w_points,
    w_out,
    w_trans,
    bias,
    wide,
    w_local,
    pair_part,
    load_sem,
    send_a,
    recv_a,
    send_b,
    recv_b,
):
    me = lax.axis_index("row")
    rows = packed.shape[0]
    count = rows * n
    lines = rows * PACK

    barrier = pltpu.get_barrier_semaphore()

    def greet(s, carry):
        pl.semaphore_signal(
            barrier, inc=1, device_id={"row": lax.rem(me + s, n)}, device_id_type=MESH
        )
        return carry

    lax.fori_loop(1, n, greet, 0)
    loads = [
        pltpu.make_async_copy(src, dst, load_sem.at[k])
        for k, (src, dst) in enumerate(
            (
                (pair_hbm, pair),
                (w_qkv_hbm, w_qkv),
                (w_points_hbm, w_points),
                (w_out_hbm, w_out),
                (w_trans_hbm, w_trans),
            )
        )
    ]
    for load in loads:
        load.start()
    pl.semaphore_wait(barrier, n - 1)

    def copy_of(s, src, dst, send, recv):
        return pltpu.make_async_remote_copy(
            src_ref=src,
            dst_ref=dst.at[pl.ds(pl.multiple_of(me * rows, rows), rows)],
            send_sem=send.at[s],
            recv_sem=recv.at[s],
            device_id={"row": lax.rem(me + s, n)},
            device_id_type=MESH,
        )

    def exchange(src, dst, send, recv):
        def go(s, carry):
            copy_of(s, src, dst, send, recv).start()
            return carry

        lax.fori_loop(1, n, go, 0)

    def settle(src, dst, send, recv):
        def go(s, carry):
            copy_of(s, src, dst, send, recv).wait()
            return carry

        lax.fori_loop(1, n, go, 0)

    exchange(packed, gathered, send_a, recv_a)
    mine = pl.ds(pl.multiple_of(me * rows, rows), rows)
    gathered[mine, :] = packed[...]

    wide[...] = jnp.zeros_like(wide)
    wide[:, :HEADS] = w_bias[...].astype(F32)
    w_bias_t = wide[...].T[:PACK].astype(BF16)
    loads[0].wait()

    def bias_row(i, carry):
        bias[pl.ds(pl.multiple_of(i * PACK, PACK), PACK), :] = dot_nt(w_bias_t, pair[i])
        return carry

    lax.fori_loop(0, rows, bias_row, 0, unroll=4)

    line = iota((lines, 1), 0)
    line_head = line % PACK
    line_row = line // PACK
    at_own = iota((lines, count), 1) == me * rows + line_row
    chain_q = jnp.sum(jnp.where(at_own, chain_ref[...], 0), 1, keepdims=True)
    mask_q = jnp.sum(jnp.where(at_own, mask_ref[...], 0), 1, keepdims=True)
    at_head = iota((lines, HEADS), 1) == line_head
    gamma = jnp.sum(jnp.where(at_head, jax.nn.softplus(head_weights[...]), 0.0), 1, keepdims=True)
    chain_add = jnp.sum(jnp.where(at_head, chain_bias[...], 0.0), 1, keepdims=True)
    column = iota((lines, WIDTH), 1)
    of_head = column // HEAD_DIM == line_head
    of_key = of_head & (column % POINTS >= QK_POINTS) & (column % POINTS < 2 * QK_POINTS)
    of_value = of_head & (column % POINTS >= 2 * QK_POINTS)
    spread = (iota((lines, rows), 1) == line_row).astype(BF16)
    same = (chain_q == chain_ref[...]).astype(F32)
    pair_mask = (mask_q * mask_ref[...]).astype(F32)
    bias[...] = bias[...] * math.sqrt(1.0 / 3.0) + (
        chain_add * same + mask_bias * (pair_mask - 1.0)
    )

    loads[1].wait()
    loads[2].wait()
    nodes = packed[:, :-FRAME]
    rotate, trans = frames(packed[:, -FRAME:].astype(F32))
    query = dot(nodes, w_qkv[:, :WIDTH]).astype(BF16)
    own_points = spatial_points(nodes, rotate, trans, w_points)
    q_lines = jnp.where(of_head, dot(spread, query), 0.0).astype(BF16)
    p_lines = [
        jnp.where(of_key, pltpu.roll(dot(spread, own_points[a]), QK_POINTS, 1), 0.0)
        for a in range(3)
    ]
    q_square = sum(jnp.sum(p * p, 1, keepdims=True) for p in p_lines)
    p_lines = [(-2.0 * p).astype(BF16) for p in p_lines]
    ones_key = of_key.astype(BF16)

    loads[3].wait()
    for k in range(4):
        start = WIDTH + k * HEADS * V_POINTS
        block = w_out[start : start + HEADS * V_POINTS, :].astype(F32)
        block = block.reshape(HEADS, V_POINTS, -1)
        block = jnp.concatenate([jnp.zeros_like(block), block], 1)
        w_local[k] = block.reshape(WIDTH, -1).astype(BF16)

    settle(packed, gathered, send_a, recv_a)

    every = gathered[:, :-FRAME]
    key = dot(every, w_qkv[:, WIDTH : 2 * WIDTH]).astype(BF16)
    value = dot(every, w_qkv[:, 2 * WIDTH :]).astype(BF16)
    rotate_all, trans_all = frames(gathered[:, -FRAME:].astype(F32))
    points = spatial_points(every, rotate_all, trans_all, w_points)
    square = sum(p.astype(F32) * p.astype(F32) for p in points)
    high = square.astype(BF16)
    rest = square - high.astype(F32)
    middle = rest.astype(BF16)
    low = (rest - middle.astype(F32)).astype(BF16)
    dots = dot_nt(q_lines, key)
    distance = q_square + (
        dot_nt(p_lines[0], points[0])
        + dot_nt(p_lines[1], points[1])
        + dot_nt(p_lines[2], points[2])
        + dot_nt(ones_key, high)
        + dot_nt(ones_key, middle)
        + dot_nt(ones_key, low)
    )
    weight_c = math.sqrt(2.0 / (9.0 * QK_POINTS))
    third = math.sqrt(1.0 / 3.0)
    logit = (
        dots * (third / math.sqrt(HEAD_DIM)) - (0.5 * weight_c * third) * gamma * distance
    ) + bias[...]
    expo = jnp.exp(logit - jnp.max(logit, 1, keepdims=True))
    inverse = 1.0 / jnp.sum(expo, 1, keepdims=True)
    weights = expo.astype(BF16)

    def collect(lines_value, keep):
        kept = jnp.where(keep, lines_value * inverse, 0.0)
        return jnp.sum(kept.reshape(rows, PACK, WIDTH), 1)

    for i in range(rows):
        part = slice(i * PACK, (i + 1) * PACK)
        pair_part[part, :] = dot(weights[part], pair[i]) * inverse[part]
    node_part = collect(dot(weights, value), of_head)
    shifted = [collect(dot(weights, points[a]), of_value) - trans[a] for a in range(3)]
    local = [
        rotate[0][a] * shifted[0] + rotate[1][a] * shifted[1] + rotate[2][a] * shifted[2]
        for a in range(3)
    ]
    length = jnp.sqrt(
        local[0] * local[0] + local[1] * local[1] + local[2] * local[2] + point_eps
    )
    wide_part = jnp.concatenate(
        [pair_part[pl.ds(h, rows, stride=PACK), :] for h in range(HEADS)], 1
    ).astype(BF16)
    loads[4].wait()
    update = dot(node_part.astype(BF16), w_out[:WIDTH, :]) + b_out[...]
    for k, part in enumerate(local + [length]):
        update = update + dot(part.astype(BF16), w_local[k])
    update = update + dot(wide_part, w_out[WIDTH + 4 * HEADS * V_POINTS :, :])
    first = layer_norm(nodes.astype(F32) + update).astype(BF16)
    hidden = jnp.maximum(dot(first, w_trans[0]), 0.0).astype(BF16)
    hidden = jnp.maximum(dot(hidden, w_trans[1]), 0.0).astype(BF16)
    last = dot(hidden, w_trans[2])
    own_line = iota((rows, count), 1) == me * rows + iota((rows, count), 0)
    own_mask = jnp.sum(jnp.where(own_line, mask_ref[...], 0), 1, keepdims=True)
    result = (layer_norm(first.astype(F32) + last) * own_mask.astype(F32)).astype(BF16)
    own_end[...] = dot(result, w_edge_node[...]).astype(BF16)
    exchange(own_end, ends, send_b, recv_b)
    node_out[...] = result
    own_out[...] = own_end[...].astype(F32)
    ends[mine, :] = own_end[...]
    settle(own_end, ends, send_b, recv_b)
    ends_out[...] = ends[...]


def edge_kernel(
    step_rows,
    pair,
    ends,
    own,
    mask_ref,
    w_in,
    b_in,
    w_mid,
    b_mid,
    w_last,
    b_last,
    out,
    near,
    mask_cols,
    w_first,
):
    me = lax.axis_index("row")
    step = pl.program_id(0)
    count = ends.shape[0]
    rows = own.shape[0]
    c = C_PAIR

    @pl.when(step == 0)
    def _():
        near[...] = dot(own[...].astype(BF16), w_in[c : c + EDGE_NODE, :]) + b_in[...]
        eye = iota((count, count), 0) == iota((count, count), 1)
        line = jnp.sum(jnp.where(eye, mask_ref[...], 0), 1, keepdims=True).astype(F32)
        mask_cols[...] = jnp.broadcast_to(line, mask_cols.shape)
        w_first[:c, :] = w_in[:c, :]
        w_first[c:, :] = w_in[c + EDGE_NODE :, :]

    far = ends[...]
    for r in range(step_rows):
        i = step * step_rows + r
        row = pair[r]
        near_row = near[pl.ds(i, 1), :]
        own_row = own[pl.ds(i, 1), :]
        mask_row = mask_cols[pl.ds(me * rows + i, 1), :]
        pre = dot(jnp.concatenate([row, far], 1), w_first[...]) + near_row
        first = jnp.maximum(pre.astype(BF16), 0.0)
        second = jnp.maximum(dot(first, w_mid[...]) + b_mid[...], 0.0)
        resid = jnp.concatenate(
            [
                second[:, :c] + row.astype(F32),
                second[:, c : c + EDGE_NODE] + own_row,
                second[:, c + EDGE_NODE :] + far.astype(F32),
            ],
            1,
        ).astype(BF16)
        last = dot(resid, w_last[...]) + b_last[...]
        out[r] = (layer_norm(last) * (mask_row * mask_cols[...])).astype(BF16)


def body(
    n,
    node_feats,
    pair_feats,
    trans,
    frame_seed,
    residue_mask,
    chain_index,
    w_qkv,
    w_points,
    w_bias,
    head_weights,
    chain_bias,
    w_out,
    b_out,
    w_trans,
    w_edge_node,
    w_edge_in,
    b_edge_in,
    w_edge_mid,
    b_edge_mid,
    w_edge_out,
    b_edge_out,
):
    rows, d_node = node_feats.shape
    count = rows * n
    lines = rows * PACK
    pad = jnp.zeros((rows, FRAME - 6), BF16)
    packed = jnp.concatenate([node_feats, trans, frame_seed.astype(BF16), pad], 1)
    mask_line = residue_mask[None]
    vmem = pl.BlockSpec(memory_space=pltpu.VMEM)
    hbm = pl.BlockSpec(memory_space=pl.ANY)
    node_out, ends, own = pl.pallas_call(
        functools.partial(node_kernel, n),
        out_shape=(
            jax.ShapeDtypeStruct((rows, d_node), BF16),
            jax.ShapeDtypeStruct((count, EDGE_NODE), BF16),
            jax.ShapeDtypeStruct((rows, EDGE_NODE), F32),
        ),
        in_specs=[vmem] * 8 + [hbm] * 5,
        out_specs=(vmem, vmem, vmem),
        scratch_shapes=[
            pltpu.VMEM((count, d_node + FRAME), BF16),
            pltpu.VMEM((count, EDGE_NODE), BF16),
            pltpu.VMEM((rows, EDGE_NODE), BF16),
            pltpu.VMEM(pair_feats.shape, BF16),
            pltpu.VMEM(w_qkv.shape, BF16),
            pltpu.VMEM(w_points.shape, BF16),
            pltpu.VMEM(w_out.shape, BF16),
            pltpu.VMEM(w_trans.shape, BF16),
            pltpu.VMEM((lines, count), F32),
            pltpu.VMEM((C_PAIR, 128), F32),
            pltpu.VMEM((4, WIDTH, d_node), BF16),
            pltpu.VMEM((lines, C_PAIR), F32),
            pltpu.SemaphoreType.DMA((5,)),
            pltpu.SemaphoreType.DMA((n,)),
            pltpu.SemaphoreType.DMA((n,)),
            pltpu.SemaphoreType.DMA((n,)),
            pltpu.SemaphoreType.DMA((n,)),
        ],
        compiler_params=pltpu.CompilerParams(
            collective_id=0, has_side_effects=True, vmem_limit_bytes=VMEM_LIMIT
        ),
        name="node",
    )(
        packed,
        mask_line,
        chain_index[None],
        w_bias,
        head_weights[None],
        chain_bias[None],
        b_out[None],
        w_edge_node,
        pair_feats,
        w_qkv,
        w_points,
        w_out,
        w_trans,
    )
    step_rows = 2 if count <= 512 else 1

    def fixed(array):
        return pl.BlockSpec(array.shape, lambda s: (0,) * array.ndim)

    constants = (
        ends,
        own,
        mask_line,
        w_edge_in,
        b_edge_in[None],
        w_edge_mid,
        b_edge_mid[None],
        w_edge_out,
        b_edge_out[None],
    )
    block = pl.BlockSpec((step_rows, count, C_PAIR), lambda s: (s, 0, 0))
    pair_out = pl.pallas_call(
        functools.partial(edge_kernel, step_rows),
        out_shape=jax.ShapeDtypeStruct(pair_feats.shape, BF16),
        grid=(rows // step_rows,),
        in_specs=[block] + [fixed(array) for array in constants],
        out_specs=block,
        scratch_shapes=[
            pltpu.VMEM((rows, w_edge_in.shape[1]), F32),
            pltpu.VMEM((count, C_PAIR), F32),
            pltpu.VMEM((C_PAIR + EDGE_NODE, w_edge_in.shape[1]), BF16),
        ],
        compiler_params=pltpu.CompilerParams(vmem_limit_bytes=VMEM_LIMIT),
        name="edge",
    )(pair_feats, *constants)
    return (node_out, pair_out)


def solution(mesh):
    split = P(("grp", "row"), None)
    in_specs = (
        split,
        P(("grp", "row"), None, None),
        split,
        split,
        P("grp"),
        P("grp"),
    ) + (P(),) * 15
    out_specs = (split, P(("grp", "row"), None, None))
    return jax.shard_map(
        functools.partial(body, mesh.shape["row"]),
        mesh=mesh,
        in_specs=in_specs,
        out_specs=out_specs,
        check_vma=False,
    )
```

time: 139 us -> 45.5 us (0.33)
  blocking collectives: 60.9 us -> 0 us
  Pallas kernels: 0 us -> 33.2 us
  matrix products: 32 us -> 0 us
  local copies, waits for them, and re-layouts: 27.6 us -> 9.12 us
  other arithmetic: 15.4 us -> 2.06 us
    all_gather x3 -> x0, blocking collectives: 60.9 us -> none  [the longest x1 24 us: body(): lax.all_gather(projected[1], 'row', axis=0, tiled=True)]
    pallas_call x0 -> x2, Pallas kernels: none -> 33.2 us  [the longest x1 21.9 us: body(): pl.pallas_call(functools.partial(node_kernel, n), out_shape=(jax.ShapeDty...]
    dot_general x50 -> x0, matrix products: 32 us -> none  [the longest x16 22.2 us: one_row(): jnp.dot(first, w_edge_mid, preferred_element_type=jnp.float32) + b_edge_mid]
    dynamic_update_slice x32 -> x0, local copies, waits for them, and re-layouts: 12 us -> none  [body(): pair_out = lax.map(one_row, (pair_block, near, endpoint, mask_rows))]
    dynamic_slice x33 -> x0, local copies, waits for them, and re-layouts: 11.2 us -> none  [the longest x32 11.1 us: body(): pair_out = lax.map(one_row, (pair_block, near, endpoint, mask_rows))]
    sqrt x19 -> x0, other arithmetic: 11.2 us -> none  [the longest x18 11.1 us: layer_norm(): jnp.sqrt(jnp.mean(centred * centred, -1, keepdims=True) + norm_eps)]
    unnamed x40 -> x7, local copies, waits for them, and re-layouts: 0.46 us -> 6.48 us
    broadcast_in_dim x16 -> x3, local copies, waits for them, and re-layouts: 0.13 us -> 2.47 us  [the longest x1 1.24 us: body(): b_edge_in[None]]
where the time goes in v1:
time: 45.5 us; the launch traced here: 45.1 us
  Pallas kernels  33.2 us (73%)
  local copies, waits for them, and re-layouts  9.12 us (20%)
  other arithmetic  2.06 us (5%)
  between operations  0.66 us (1%)
    pallas_call x1, Pallas kernels, body(): pl.pallas_call(functools.partial(node_kernel, n), out_shape=(jax.ShapeDty...  21.9 us
    pallas_call x1, Pallas kernels, body(): pl.pallas_call(functools.partial(edge_kernel, step_rows), out_shape=jax.S...  11.4 us
    unnamed x7, local copies, waits for them, and re-layouts  6.48 us
    concatenate x1, other arithmetic, body(): jnp.concatenate([node_feats, trans, frame_seed.astype(BF16), pad], 1)  1.37 us
    broadcast_in_dim x1, local copies, waits for them, and re-layouts, body(): b_edge_in[None]  1.24 us
    broadcast_in_dim x1, local copies, waits for them, and re-layouts, body(): b_edge_mid[None]  1.23 us

profile of v1, /device:TPU:0, one launch (start us, length us, event | category | flops | bytes accessed | tf_op | source)
XLA Modules:
  0.0 45.1 jit_solution(15872892632768009739)
XLA Ops:
  0.6 0.1 pad.3.clone
  0.7 0.7 %convert_element_type.3 = bf16[16,3]{0,1:T(4,128)(2,1)S(1)} convert(s32[16,3]{0,1:T(4,128)} %param.24) | non-fusion elementwise | flops 48 | bytes 288 | tf_op jit(solution)/shard_map/convert_element_type | solution.py:382
  1.4 1.2 %broadcast_in_dim.33.b_in = f32[1,384]{1,0:T(1,128)} reshape(f32[384]{0:T(512)} %param.37) | data formatting | bytes 3072 | tf_op jit(solution)/shard_map/broadcast_in_dim | solution.py:443
  2.6 1.2 %broadcast_in_dim.34.b_mid = f32[1,384]{1,0:T(1,128)} reshape(f32[384]{0:T(512)} %param.39) | data formatting | bytes 3072 | tf_op jit(solution)/shard_map/broadcast_in_dim | solution.py:445
  3.9 0.1 copy.29
  4.0 0.8 %copy.28 = bf16[16,3]{1,0:T(8,128)(2,1)S(1)} copy(bf16[16,3]{0,1:T(4,128)(2,1)} %param.23) | data formatting | bytes 192 | tf_op args[2]
  4.7 1.4 %maximum_maximum_fusion.packed = bf16[16,384]{1,0:T(8,128)(2,1)} fusion(bf16[16,3]{1,0:T(8,128)(2,1)S(1)} %copy.29, bf16[16,3]{1,0:T(8,128)(2,1)S(1)} %copy.28, bf16[16,256]{1,0:T(8,128)(2,1)} %param.21, bf16[384]{0:T(512)(128)(2,1)S(1)} %pad.3.clone), kind=kLoop, calls=%fused_computation | loop fusion | flops 49152 | bytes 21440 | tf_op jit(solution)/shard_map/concatenate | solution.py:382
  6.1 1.4 %copy.30.w_bias = bf16[128,12]{1,0:T(8,128)(2,1)} copy(bf16[128,12]{0,1:T(8,128)(2,1)} %param.29) | data formatting | bytes 6144 | tf_op args[8]
  7.5 1.9 %copy.31.w_qkv_hbm = bf16[256,576]{1,0:T(8,128)(2,1)} copy(bf16[256,576]{0,1:T(8,128)(2,1)} %param.27) | data formatting | bytes 589824 | tf_op args[6]
  9.4 1.9 %copy.32.w_points_hbm = bf16[256,576]{1,0:T(8,128)(2,1)} copy(bf16[256,576]{0,1:T(8,128)(2,1)} %param.28) | data formatting | bytes 589824 | tf_op args[7]
  11.2 21.9 %node.1 = (bf16[16,256]{1,0:T(8,128)(2,1)}, bf16[256,128]{1,0:T(8,128)(2,1)}, f32[16,128]{1,0:T(8,128)}) custom-call(bf16[16,384]{1,0:T(8,128)(2,1)} %maximum_maximum_fusion.packed, s32[1,256]{1,0:T(1,128)} %bitcast.6, s32[1,256]{1,0:T(1,128)} %bitcast.8, bf16[128,12]{1,0:T(8,128)(2,1)} %copy.30.w_bias, f32[1,12]{1,0:T(1,128)} %bitcast.10, ...), custom_call_target="tpu_custom_call" | custom-call | tf_op jit(solution)/shard_map/node/pallas_call | solution.py:386
  33.1 0.0 copy-start
  33.1 11.4 %edge.1 = bf16[16,256,128]{2,1,0:T(8,128)(2,1)} custom-call(bf16[16,256,128]{2,1,0:T(8,128)(2,1)} %pair.1, bf16[256,128]{1,0:T(8,128)(2,1)} %get-tuple-element.6.ends, f32[16,128]{1,0:T(8,128)} %get-tuple-element.7.own, s32[1,256]{1,0:T(1,128)} %bitcast.7, bf16[384,384]{1,0:T(8,128)(2,1)} %w_in.1, f32[1,384]{1,0:T(1,128)} %broadcast_in_dim.33.b_in, ...), custom_call_target="tpu_custom_call" | custom-call | tf_op jit(solution)/shard_map/edge/pallas_call | solution.py:450
  44.5 0.0 copy-done
  44.5 0.6 %copy.34 = bf16[16,256]{1,0:T(8,128)(2,1)} copy(bf16[16,256]{1,0:T(8,128)(2,1)S(1)} %copy-done) | data formatting | bytes 16384
  (1 shorter events, 0.0 us)
Async XLA Ops:
  33.1 11.4 %copy-start = (bf16[16,256]{1,0:T(8,128)(2,1)S(1)}, bf16[16,256]{1,0:T(8,128)(2,1)}, u32[]{:S(2)}) copy-start(bf16[16,256]{1,0:T(8,128)(2,1)} %get-tuple-element.10) | copy-start | bytes 24580

commit v2 on v1

--- a/solution.py
+++ b/solution.py
@@ -66,7 +66,7 @@
 
 
 def spatial_points(nodes, rotate, trans, w_points):
-    local = [dot(nodes, w_points[:, b * WIDTH : (b + 1) * WIDTH]) for b in range(3)]
+    local = [dot_nt(nodes, w_points[b * WIDTH : (b + 1) * WIDTH, :]) for b in range(3)]
     return [
         (
             rotate[a][0] * local[0] + rotate[a][1] * local[1] + rotate[a][2] * local[2] + trans[a]
@@ -81,7 +81,9 @@
 
 def node_kernel(
     n,
-    packed,
+    node_feats,
+    trans_ref,
+    seed_ref,
     mask_ref,
     chain_ref,
     w_bias,
@@ -97,6 +99,7 @@
     node_out,
     ends_out,
     own_out,
+    packed,
     gathered,
     ends,
     own_end,
@@ -143,6 +146,14 @@
     ]
     for load in loads:
         load.start()
+    wide[...] = jnp.zeros_like(wide)
+    wide[:3, :rows] = trans_ref[...].astype(F32)
+    wide[3:6, :rows] = seed_ref[...].astype(F32)
+    packed[:, :-FRAME] = node_feats[...]
+    packed[:, -FRAME:] = wide[...].T[:rows].astype(BF16)
+    wide[:HEADS, :] = w_bias[...].astype(F32)
+    wide[HEADS:PACK, :] = jnp.zeros((PACK - HEADS, C_PAIR), F32)
+    w_bias_t = wide[:PACK, :].astype(BF16)
     pl.semaphore_wait(barrier, n - 1)
 
     def copy_of(s, src, dst, send, recv):
@@ -173,9 +184,6 @@
     mine = pl.ds(pl.multiple_of(me * rows, rows), rows)
     gathered[mine, :] = packed[...]
 
-    wide[...] = jnp.zeros_like(wide)
-    wide[:, :HEADS] = w_bias[...].astype(F32)
-    w_bias_t = wide[...].T[:PACK].astype(BF16)
     loads[0].wait()
 
     def bias_row(i, carry):
@@ -208,7 +216,7 @@
     loads[2].wait()
     nodes = packed[:, :-FRAME]
     rotate, trans = frames(packed[:, -FRAME:].astype(F32))
-    query = dot(nodes, w_qkv[:, :WIDTH]).astype(BF16)
+    query = dot_nt(nodes, w_qkv[:WIDTH, :]).astype(BF16)
     own_points = spatial_points(nodes, rotate, trans, w_points)
     q_lines = jnp.where(of_head, dot(spread, query), 0.0).astype(BF16)
     p_lines = [
@@ -230,8 +238,8 @@
     settle(packed, gathered, send_a, recv_a)
 
     every = gathered[:, :-FRAME]
-    key = dot(every, w_qkv[:, WIDTH : 2 * WIDTH]).astype(BF16)
-    value = dot(every, w_qkv[:, 2 * WIDTH :]).astype(BF16)
+    key = dot_nt(every, w_qkv[WIDTH : 2 * WIDTH, :]).astype(BF16)
+    value = dot_nt(every, w_qkv[2 * WIDTH :, :]).astype(BF16)
     rotate_all, trans_all = frames(gathered[:, -FRAME:].astype(F32))
     points = spatial_points(every, rotate_all, trans_all, w_points)
     square = sum(p.astype(F32) * p.astype(F32) for p in points)
@@ -302,6 +310,7 @@
     pair,
     ends,
     own,
+    nodes,
     mask_ref,
     w_in,
     b_in,
@@ -309,6 +318,7 @@
     b_mid,
     w_last,
     b_last,
+    node_out,
     out,
     near,
     mask_cols,
@@ -322,7 +332,8 @@
 
     @pl.when(step == 0)
     def _():
-        near[...] = dot(own[...].astype(BF16), w_in[c : c + EDGE_NODE, :]) + b_in[...]
+        near[...] = dot(own[...].astype(BF16), w_in[c : c + EDGE_NODE, :]) + b_in[...][None, :]
+        node_out[...] = nodes[...]
         eye = iota((count, count), 0) == iota((count, count), 1)
         line = jnp.sum(jnp.where(eye, mask_ref[...], 0), 1, keepdims=True).astype(F32)
         mask_cols[...] = jnp.broadcast_to(line, mask_cols.shape)
@@ -338,7 +349,7 @@
         mask_row = mask_cols[pl.ds(me * rows + i, 1), :]
         pre = dot(jnp.concatenate([row, far], 1), w_first[...]) + near_row
         first = jnp.maximum(pre.astype(BF16), 0.0)
-        second = jnp.maximum(dot(first, w_mid[...]) + b_mid[...], 0.0)
+        second = jnp.maximum(dot(first, w_mid[...]) + b_mid[...][None, :], 0.0)
         resid = jnp.concatenate(
             [
                 second[:, :c] + row.astype(F32),
@@ -378,31 +389,30 @@
     rows, d_node = node_feats.shape
     count = rows * n
     lines = rows * PACK
-    pad = jnp.zeros((rows, FRAME - 6), BF16)
-    packed = jnp.concatenate([node_feats, trans, frame_seed.astype(BF16), pad], 1)
     mask_line = residue_mask[None]
     vmem = pl.BlockSpec(memory_space=pltpu.VMEM)
     hbm = pl.BlockSpec(memory_space=pl.ANY)
-    node_out, ends, own = pl.pallas_call(
+    nodes, ends, own = pl.pallas_call(
         functools.partial(node_kernel, n),
         out_shape=(
             jax.ShapeDtypeStruct((rows, d_node), BF16),
             jax.ShapeDtypeStruct((count, EDGE_NODE), BF16),
             jax.ShapeDtypeStruct((rows, EDGE_NODE), F32),
         ),
-        in_specs=[vmem] * 8 + [hbm] * 5,
+        in_specs=[vmem] * 10 + [hbm] * 5,
         out_specs=(vmem, vmem, vmem),
         scratch_shapes=[
+            pltpu.VMEM((rows, d_node + FRAME), BF16),
             pltpu.VMEM((count, d_node + FRAME), BF16),
             pltpu.VMEM((count, EDGE_NODE), BF16),
             pltpu.VMEM((rows, EDGE_NODE), BF16),
             pltpu.VMEM(pair_feats.shape, BF16),
-            pltpu.VMEM(w_qkv.shape, BF16),
-            pltpu.VMEM(w_points.shape, BF16),
+            pltpu.VMEM(w_qkv.shape[::-1], BF16),
+            pltpu.VMEM(w_points.shape[::-1], BF16),
             pltpu.VMEM(w_out.shape, BF16),
             pltpu.VMEM(w_trans.shape, BF16),
             pltpu.VMEM((lines, count), F32),
-            pltpu.VMEM((C_PAIR, 128), F32),
+            pltpu.VMEM((FRAME, FRAME), F32),
             pltpu.VMEM((4, WIDTH, d_node), BF16),
             pltpu.VMEM((lines, C_PAIR), F32),
             pltpu.SemaphoreType.DMA((5,)),
@@ -416,17 +426,19 @@
         ),
         name="node",
     )(
-        packed,
+        node_feats,
+        trans.T,
+        frame_seed.T,
         mask_line,
         chain_index[None],
-        w_bias,
+        w_bias.T,
         head_weights[None],
         chain_bias[None],
         b_out[None],
         w_edge_node,
         pair_feats,
-        w_qkv,
-        w_points,
+        w_qkv.T,
+        w_points.T,
         w_out,
         w_trans,
     )
@@ -438,21 +450,25 @@
     constants = (
         ends,
         own,
+        nodes,
         mask_line,
         w_edge_in,
-        b_edge_in[None],
+        b_edge_in,
         w_edge_mid,
-        b_edge_mid[None],
+        b_edge_mid,
         w_edge_out,
         b_edge_out[None],
     )
     block = pl.BlockSpec((step_rows, count, C_PAIR), lambda s: (s, 0, 0))
-    pair_out = pl.pallas_call(
+    return pl.pallas_call(
         functools.partial(edge_kernel, step_rows),
-        out_shape=jax.ShapeDtypeStruct(pair_feats.shape, BF16),
+        out_shape=(
+            jax.ShapeDtypeStruct((rows, d_node), BF16),
+            jax.ShapeDtypeStruct(pair_feats.shape, BF16),
+        ),
         grid=(rows // step_rows,),
         in_specs=[block] + [fixed(array) for array in constants],
-        out_specs=block,
+        out_specs=(fixed(nodes), block),
         scratch_shapes=[
             pltpu.VMEM((rows, w_edge_in.shape[1]), F32),
             pltpu.VMEM((count, C_PAIR), F32),
@@ -461,7 +477,6 @@
         compiler_params=pltpu.CompilerParams(vmem_limit_bytes=VMEM_LIMIT),
         name="edge",
     )(pair_feats, *constants)
-    return (node_out, pair_out)
 
 
 def solution(mesh):

time: 45.5 us -> 34.3 us (0.75)
  local copies, waits for them, and re-layouts: 9.12 us -> 0 us
  other arithmetic: 2.06 us -> 0 us
    unnamed x7 -> x0, local copies, waits for them, and re-layouts: 6.48 us -> none
    broadcast_in_dim x3 -> x0, local copies, waits for them, and re-layouts: 2.47 us -> none  [the longest x1 1.24 us: body(): b_edge_in[None]]
    concatenate x1 -> x0, other arithmetic: 1.37 us -> none  [body(): jnp.concatenate([node_feats, trans, frame_seed.astype(BF16), pad], 1)]
    convert_element_type x1 -> x0, other arithmetic: 0.68 us -> none  [body(): frame_seed.astype(BF16)]
where the time goes in v2:
time: 34.3 us; the launch traced here: 34.1 us
  Pallas kernels  33.4 us (97%)
  between operations  0.64 us (2%)
    pallas_call x1, Pallas kernels, body(): pl.pallas_call(functools.partial(node_kernel, n), out_shape=(jax.ShapeDty...  21.9 us
    pallas_call x1, Pallas kernels, body(): pl.pallas_call(functools.partial(edge_kernel, step_rows), out_shape=(jax....  11.5 us

profile of v2, /device:TPU:0, one launch (start us, length us, event | category | flops | bytes accessed | tf_op | source)
XLA Modules:
  0.0 34.1 jit_solution(14733675070842707626)
XLA Ops:
  0.6 21.9 %node.1 = (bf16[16,256]{1,0:T(8,128)(2,1)}, bf16[256,128]{1,0:T(8,128)(2,1)}, f32[16,128]{1,0:T(8,128)}) custom-call(bf16[16,256]{1,0:T(8,128)(2,1)} %node_feats.1, bf16[3,16]{1,0:T(4,128)(2,1)} %bitcast.17, s32[3,16]{1,0:T(4,128)} %bitcast.16, s32[1,256]{1,0:T(1,128)} %bitcast.13, s32[1,256]{1,0:T(1,128)} %bitcast.18, bf16[12,128]{1,0:T(8,128)(2,1)} %bitcast.15, ...), custom_call_target="tpu_custom_call" | custom-call | tf_op jit(solution)/shard_map/node/pallas_call | solution.py:395
  22.6 11.5 %edge.1 = (bf16[16,256]{1,0:T(8,128)(2,1)}, bf16[16,256,128]{2,1,0:T(8,128)(2,1)}) custom-call(bf16[16,256,128]{2,1,0:T(8,128)(2,1)} %pair.1, bf16[256,128]{1,0:T(8,128)(2,1)} %get-tuple-element.5.ends, f32[16,128]{1,0:T(8,128)} %get-tuple-element.6.own, bf16[16,256]{1,0:T(8,128)(2,1)} %get-tuple-element.7.nodes, s32[1,256]{1,0:T(1,128)} %bitcast.14, ...), custom_call_target="tpu_custom_call" | custom-call | tf_op jit(solution)/shard_map/edge/pallas_call | solution.py:463

commit v3 on v2

--- a/solution.py
+++ b/solution.py
@@ -96,9 +96,11 @@
     w_points_hbm,
     w_out_hbm,
     w_trans_hbm,
+    w_in_hbm,
     node_out,
     ends_out,
     own_out,
+    pre_hbm,
     packed,
     gathered,
     ends,
@@ -108,6 +110,8 @@
     w_points,
     w_out,
     w_trans,
+    w_in,
+    pre,
     bias,
     wide,
     w_local,
@@ -141,6 +145,7 @@
                 (w_points_hbm, w_points),
                 (w_out_hbm, w_out),
                 (w_trans_hbm, w_trans),
+                (w_in_hbm.at[pl.ds(0, C_PAIR)], w_in),
             )
         )
     ]
@@ -154,7 +159,6 @@
     wide[:HEADS, :] = w_bias[...].astype(F32)
     wide[HEADS:PACK, :] = jnp.zeros((PACK - HEADS, C_PAIR), F32)
     w_bias_t = wide[:PACK, :].astype(BF16)
-    pl.semaphore_wait(barrier, n - 1)
 
     def copy_of(s, src, dst, send, recv):
         return pltpu.make_async_remote_copy(
@@ -180,7 +184,6 @@
 
         lax.fori_loop(1, n, go, 0)
 
-    exchange(packed, gathered, send_a, recv_a)
     mine = pl.ds(pl.multiple_of(me * rows, rows), rows)
     gathered[mine, :] = packed[...]
 
@@ -235,6 +238,17 @@
         block = jnp.concatenate([jnp.zeros_like(block), block], 1)
         w_local[k] = block.reshape(WIDTH, -1).astype(BF16)
 
+    pl.semaphore_wait(barrier, n - 1)
+    exchange(packed, gathered, send_a, recv_a)
+    loads[5].wait()
+
+    def pair_row(i, carry):
+        pre[i] = dot(pair[i], w_in[...]).astype(BF16)
+        return carry
+
+    lax.fori_loop(0, rows, pair_row, 0, unroll=2)
+    put_pre = pltpu.make_async_copy(pre, pre_hbm, load_sem.at[6])
+    put_pre.start()
     settle(packed, gathered, send_a, recv_a)
 
     every = gathered[:, :-FRAME]
@@ -303,11 +317,13 @@
     ends[mine, :] = own_end[...]
     settle(own_end, ends, send_b, recv_b)
     ends_out[...] = ends[...]
+    put_pre.wait()
 
 
 def edge_kernel(
     step_rows,
     pair,
+    pre0,
     ends,
     own,
     nodes,
@@ -322,7 +338,7 @@
     out,
     near,
     mask_cols,
-    w_first,
+    far_in,
 ):
     me = lax.axis_index("row")
     step = pl.program_id(0)
@@ -337,8 +353,7 @@
         eye = iota((count, count), 0) == iota((count, count), 1)
         line = jnp.sum(jnp.where(eye, mask_ref[...], 0), 1, keepdims=True).astype(F32)
         mask_cols[...] = jnp.broadcast_to(line, mask_cols.shape)
-        w_first[:c, :] = w_in[:c, :]
-        w_first[c:, :] = w_in[c + EDGE_NODE :, :]
+        far_in[...] = dot(ends[...], w_in[c + EDGE_NODE :, :])
 
     far = ends[...]
     for r in range(step_rows):
@@ -347,7 +362,7 @@
         near_row = near[pl.ds(i, 1), :]
         own_row = own[pl.ds(i, 1), :]
         mask_row = mask_cols[pl.ds(me * rows + i, 1), :]
-        pre = dot(jnp.concatenate([row, far], 1), w_first[...]) + near_row
+        pre = pre0[r].astype(F32) + (far_in[...] + near_row)
         first = jnp.maximum(pre.astype(BF16), 0.0)
         second = jnp.maximum(dot(first, w_mid[...]) + b_mid[...][None, :], 0.0)
         resid = jnp.concatenate(
@@ -392,15 +407,16 @@
     mask_line = residue_mask[None]
     vmem = pl.BlockSpec(memory_space=pltpu.VMEM)
     hbm = pl.BlockSpec(memory_space=pl.ANY)
-    nodes, ends, own = pl.pallas_call(
+    nodes, ends, own, pre = pl.pallas_call(
         functools.partial(node_kernel, n),
         out_shape=(
             jax.ShapeDtypeStruct((rows, d_node), BF16),
             jax.ShapeDtypeStruct((count, EDGE_NODE), BF16),
             jax.ShapeDtypeStruct((rows, EDGE_NODE), F32),
+            jax.ShapeDtypeStruct((rows, count, w_edge_in.shape[1]), BF16),
         ),
-        in_specs=[vmem] * 10 + [hbm] * 5,
-        out_specs=(vmem, vmem, vmem),
+        in_specs=[vmem] * 10 + [hbm] * 6,
+        out_specs=(vmem, vmem, vmem, hbm),
         scratch_shapes=[
             pltpu.VMEM((rows, d_node + FRAME), BF16),
             pltpu.VMEM((count, d_node + FRAME), BF16),
@@ -411,11 +427,13 @@
             pltpu.VMEM(w_points.shape[::-1], BF16),
             pltpu.VMEM(w_out.shape, BF16),
             pltpu.VMEM(w_trans.shape, BF16),
+            pltpu.VMEM((C_PAIR, w_edge_in.shape[1]), BF16),
+            pltpu.VMEM((rows, count, w_edge_in.shape[1]), BF16),
             pltpu.VMEM((lines, count), F32),
             pltpu.VMEM((FRAME, FRAME), F32),
             pltpu.VMEM((4, WIDTH, d_node), BF16),
             pltpu.VMEM((lines, C_PAIR), F32),
-            pltpu.SemaphoreType.DMA((5,)),
+            pltpu.SemaphoreType.DMA((7,)),
             pltpu.SemaphoreType.DMA((n,)),
             pltpu.SemaphoreType.DMA((n,)),
             pltpu.SemaphoreType.DMA((n,)),
@@ -441,6 +459,7 @@
         w_points.T,
         w_out,
         w_trans,
+        w_edge_in,
     )
     step_rows = 2 if count <= 512 else 1
 
@@ -460,6 +479,7 @@
         b_edge_out[None],
     )
     block = pl.BlockSpec((step_rows, count, C_PAIR), lambda s: (s, 0, 0))
+    wide_block = pl.BlockSpec((step_rows,) + pre.shape[1:], lambda s: (s, 0, 0))
     return pl.pallas_call(
         functools.partial(edge_kernel, step_rows),
         out_shape=(
@@ -467,16 +487,16 @@
             jax.ShapeDtypeStruct(pair_feats.shape, BF16),
         ),
         grid=(rows // step_rows,),
-        in_specs=[block] + [fixed(array) for array in constants],
+        in_specs=[block, wide_block] + [fixed(array) for array in constants],
         out_specs=(fixed(nodes), block),
         scratch_shapes=[
             pltpu.VMEM((rows, w_edge_in.shape[1]), F32),
             pltpu.VMEM((count, C_PAIR), F32),
-            pltpu.VMEM((C_PAIR + EDGE_NODE, w_edge_in.shape[1]), BF16),
+            pltpu.VMEM((count, w_edge_in.shape[1]), F32),
         ],
         compiler_params=pltpu.CompilerParams(vmem_limit_bytes=VMEM_LIMIT),
         name="edge",
-    )(pair_feats, *constants)
+    )(pair_feats, pre, *constants)
 
 
 def solution(mesh):

time: 34.3 us -> 32.9 us (0.959)
  Pallas kernels: 33.4 us -> 31.9 us
    pallas_call x1, Pallas kernels: 11.5 us -> 10 us  [body(): pl.pallas_call(functools.partial(edge_kernel, step_rows), out_shape=(jax....]
where the time goes in v3:
time: 32.9 us; the launch traced here: 32.6 us
  Pallas kernels  31.9 us (97%)
  between operations  0.64 us (2%)
    pallas_call x1, Pallas kernels, body(): pl.pallas_call(functools.partial(node_kernel, n), out_shape=(jax.ShapeDty...  21.9 us
    pallas_call x1, Pallas kernels, body(): pl.pallas_call(functools.partial(edge_kernel, step_rows), out_shape=(jax....  10 us

profile of v3, /device:TPU:0, one launch (start us, length us, event | category | flops | bytes accessed | tf_op | source)
XLA Modules:
  0.0 32.6 jit_solution(16421143816239116559)
XLA Ops:
  0.6 21.9 %node.1 = (bf16[16,256]{1,0:T(8,128)(2,1)}, bf16[256,128]{1,0:T(8,128)(2,1)}, f32[16,128]{1,0:T(8,128)}, bf16[16,256,384]{2,1,0:T(8,128)(2,1)}) custom-call(bf16[16,256]{1,0:T(8,128)(2,1)} %node_feats.1, bf16[3,16]{1,0:T(4,128)(2,1)} %bitcast.17, s32[3,16]{1,0:T(4,128)} %bitcast.16, s32[1,256]{1,0:T(1,128)} %bitcast.14, s32[1,256]{1,0:T(1,128)} %bitcast.18, ...), custom_call_target="tpu_custom_call" | custom-call | tf_op jit(solution)/shard_map/node/pallas_call | solution.py:410
  22.6 10.0 %edge.1 = (bf16[16,256]{1,0:T(8,128)(2,1)}, bf16[16,256,128]{2,1,0:T(8,128)(2,1)}) custom-call(bf16[16,256,128]{2,1,0:T(8,128)(2,1)} %pair.1, bf16[16,256,384]{2,1,0:T(8,128)(2,1)} %get-tuple-element.6.pre0, bf16[256,128]{1,0:T(8,128)(2,1)} %get-tuple-element.7.ends, f32[16,128]{1,0:T(8,128)} %get-tuple-element.8.own, ...), custom_call_target="tpu_custom_call" | custom-call | tf_op jit(solution)/shard_map/edge/pallas_call | solution.py:483

commit v4 on v3

--- a/solution.py
+++ b/solution.py
@@ -239,17 +239,67 @@
         w_local[k] = block.reshape(WIDTH, -1).astype(BF16)
 
     pl.semaphore_wait(barrier, n - 1)
-    exchange(packed, gathered, send_a, recv_a)
+    partner = me + 1 - 2 * lax.rem(me, 2)
+
+    def across(s):
+        return pltpu.make_async_remote_copy(
+            src_ref=packed,
+            dst_ref=gathered.at[mine],
+            send_sem=send_a.at[s],
+            recv_sem=recv_a.at[s],
+            device_id={"row": lax.rem(me + 2 * s, n)},
+            device_id_type=MESH,
+        )
+
+    to_partner = pltpu.make_async_remote_copy(
+        src_ref=packed,
+        dst_ref=gathered.at[mine],
+        send_sem=send_a.at[0],
+        recv_sem=recv_a.at[0],
+        device_id={"row": partner},
+        device_id_type=MESH,
+    )
+
+    def pass_on(s):
+        source = pl.ds(pl.multiple_of(lax.rem(me + n - 2 * s, n) * rows, rows), rows)
+        return pltpu.make_async_remote_copy(
+            src_ref=gathered.at[source],
+            dst_ref=gathered.at[source],
+            send_sem=send_a.at[n // 2 + s],
+            recv_sem=recv_a.at[n // 2 + s],
+            device_id={"row": partner},
+            device_id_type=MESH,
+        )
+
+    def send_across(s, carry):
+        across(s).start()
+        return carry
+
+    def relay(s, carry):
+        across(s).wait_recv()
+        pass_on(s).start()
+        return carry
+
+    def finish(s, carry):
+        across(s).wait_send()
+        pass_on(s).wait()
+        return carry
+
+    lax.fori_loop(1, n // 2, send_across, 0)
+    to_partner.start()
     loads[5].wait()
 
     def pair_row(i, carry):
         pre[i] = dot(pair[i], w_in[...]).astype(BF16)
         return carry
 
-    lax.fori_loop(0, rows, pair_row, 0, unroll=2)
+    lax.fori_loop(0, rows // 2, pair_row, 0, unroll=2)
+    lax.fori_loop(1, n // 2, relay, 0)
+    lax.fori_loop(rows // 2, rows, pair_row, 0, unroll=2)
     put_pre = pltpu.make_async_copy(pre, pre_hbm, load_sem.at[6])
     put_pre.start()
-    settle(packed, gathered, send_a, recv_a)
+    to_partner.wait()
+    lax.fori_loop(1, n // 2, finish, 0)
 
     every = gathered[:, :-FRAME]
     key = dot_nt(every, w_qkv[WIDTH : 2 * WIDTH, :]).astype(BF16)
@@ -461,7 +511,7 @@
         w_trans,
         w_edge_in,
     )
-    step_rows = 2 if count <= 512 else 1
+    step_rows = 4 if count <= 512 else 1
 
     def fixed(array):
         return pl.BlockSpec(array.shape, lambda s: (0,) * array.ndim)

time: 32.9 us -> 30.2 us (0.918)
  Pallas kernels: 31.9 us -> 29.4 us
    pallas_call x1, Pallas kernels: 10 us -> 8.02 us  [body(): pl.pallas_call(functools.partial(edge_kernel, step_rows), out_shape=(jax....]
    pallas_call x1, Pallas kernels: 21.9 us -> 21.4 us  [body(): pl.pallas_call(functools.partial(node_kernel, n), out_shape=(jax.ShapeDty...]
where the time goes in v4:
time: 30.2 us; the launch traced here: 30 us
  Pallas kernels  29.4 us (97%)
  between operations  0.64 us (2%)
    pallas_call x1, Pallas kernels, body(): pl.pallas_call(functools.partial(node_kernel, n), out_shape=(jax.ShapeDty...  21.4 us
    pallas_call x1, Pallas kernels, body(): pl.pallas_call(functools.partial(edge_kernel, step_rows), out_shape=(jax....  8.02 us

profile of v4, /device:TPU:0, one launch (start us, length us, event | category | flops | bytes accessed | tf_op | source)
XLA Modules:
  0.0 30.0 jit_solution(17738268426254902567)
XLA Ops:
  0.6 21.4 %node.1 = (bf16[16,256]{1,0:T(8,128)(2,1)}, bf16[256,128]{1,0:T(8,128)(2,1)}, f32[16,128]{1,0:T(8,128)}, bf16[16,256,384]{2,1,0:T(8,128)(2,1)}) custom-call(bf16[16,256]{1,0:T(8,128)(2,1)} %node_feats.1, bf16[3,16]{1,0:T(4,128)(2,1)} %bitcast.17, s32[3,16]{1,0:T(4,128)} %bitcast.16, s32[1,256]{1,0:T(1,128)} %bitcast.14, s32[1,256]{1,0:T(1,128)} %bitcast.18, ...), custom_call_target="tpu_custom_call" | custom-call | tf_op jit(solution)/shard_map/node/pallas_call | solution.py:460
  22.0 8.0 %edge.1 = (bf16[16,256]{1,0:T(8,128)(2,1)}, bf16[16,256,128]{2,1,0:T(8,128)(2,1)}) custom-call(bf16[16,256,128]{2,1,0:T(8,128)(2,1)} %pair.1, bf16[16,256,384]{2,1,0:T(8,128)(2,1)} %get-tuple-element.6.pre0, bf16[256,128]{1,0:T(8,128)(2,1)} %get-tuple-element.7.ends, f32[16,128]{1,0:T(8,128)} %get-tuple-element.8.own, ...), custom_call_target="tpu_custom_call" | custom-call | tf_op jit(solution)/shard_map/edge/pallas_call | solution.py:533

commit v5 on v4

--- a/solution.py
+++ b/solution.py
@@ -215,6 +215,56 @@
         chain_add * same + mask_bias * (pair_mask - 1.0)
     )
 
+    pl.semaphore_wait(barrier, n - 1)
+    partner = me + 1 - 2 * lax.rem(me, 2)
+
+    def across(s):
+        return pltpu.make_async_remote_copy(
+            src_ref=packed,
+            dst_ref=gathered.at[mine],
+            send_sem=send_a.at[s],
+            recv_sem=recv_a.at[s],
+            device_id={"row": lax.rem(me + 2 * s, n)},
+            device_id_type=MESH,
+        )
+
+    to_partner = pltpu.make_async_remote_copy(
+        src_ref=packed,
+        dst_ref=gathered.at[mine],
+        send_sem=send_a.at[0],
+        recv_sem=recv_a.at[0],
+        device_id={"row": partner},
+        device_id_type=MESH,
+    )
+
+    def pass_on(s):
+        source = pl.ds(pl.multiple_of(lax.rem(me + n - 2 * s, n) * rows, rows), rows)
+        return pltpu.make_async_remote_copy(
+            src_ref=gathered.at[source],
+            dst_ref=gathered.at[source],
+            send_sem=send_a.at[n // 2 + s],
+            recv_sem=recv_a.at[n // 2 + s],
+            device_id={"row": partner},
+            device_id_type=MESH,
+        )
+
+    def send_across(s, carry):
+        across(s).start()
+        return carry
+
+    def relay(s, carry):
+        across(s).wait_recv()
+        pass_on(s).start()
+        return carry
+
+    def finish(s, carry):
+        across(s).wait_send()
+        pass_on(s).wait()
+        return carry
+
+    lax.fori_loop(1, n // 2, send_across, 0)
+    to_partner.start()
+
     loads[1].wait()
     loads[2].wait()
     nodes = packed[:, :-FRAME]
@@ -238,66 +288,22 @@
         block = jnp.concatenate([jnp.zeros_like(block), block], 1)
         w_local[k] = block.reshape(WIDTH, -1).astype(BF16)
 
-    pl.semaphore_wait(barrier, n - 1)
-    partner = me + 1 - 2 * lax.rem(me, 2)
-
-    def across(s):
-        return pltpu.make_async_remote_copy(
-            src_ref=packed,
-            dst_ref=gathered.at[mine],
-            send_sem=send_a.at[s],
-            recv_sem=recv_a.at[s],
-            device_id={"row": lax.rem(me + 2 * s, n)},
-            device_id_type=MESH,
-        )
-
-    to_partner = pltpu.make_async_remote_copy(
-        src_ref=packed,
-        dst_ref=gathered.at[mine],
-        send_sem=send_a.at[0],
-        recv_sem=recv_a.at[0],
-        device_id={"row": partner},
-        device_id_type=MESH,
-    )
-
-    def pass_on(s):
-        source = pl.ds(pl.multiple_of(lax.rem(me + n - 2 * s, n) * rows, rows), rows)
-        return pltpu.make_async_remote_copy(
-            src_ref=gathered.at[source],
-            dst_ref=gathered.at[source],
-            send_sem=send_a.at[n // 2 + s],
-            recv_sem=recv_a.at[n // 2 + s],
-            device_id={"row": partner},
-            device_id_type=MESH,
-        )
-
-    def send_across(s, carry):
-        across(s).start()
-        return carry
-
-    def relay(s, carry):
-        across(s).wait_recv()
-        pass_on(s).start()
-        return carry
-
-    def finish(s, carry):
-        across(s).wait_send()
-        pass_on(s).wait()
-        return carry
-
-    lax.fori_loop(1, n // 2, send_across, 0)
-    to_partner.start()
     loads[5].wait()
 
     def pair_row(i, carry):
         pre[i] = dot(pair[i], w_in[...]).astype(BF16)
         return carry
 
-    lax.fori_loop(0, rows // 2, pair_row, 0, unroll=2)
+    half = rows // 2
+    puts = [
+        pltpu.make_async_copy(
+            pre.at[pl.ds(k * half, half)], pre_hbm.at[pl.ds(k * half, half)], load_sem.at[6 + k]
+        )
+        for k in range(2)
+    ]
     lax.fori_loop(1, n // 2, relay, 0)
-    lax.fori_loop(rows // 2, rows, pair_row, 0, unroll=2)
-    put_pre = pltpu.make_async_copy(pre, pre_hbm, load_sem.at[6])
-    put_pre.start()
+    lax.fori_loop(0, half, pair_row, 0, unroll=2)
+    puts[0].start()
     to_partner.wait()
     lax.fori_loop(1, n // 2, finish, 0)
 
@@ -363,11 +369,14 @@
     own_end[...] = dot(result, w_edge_node[...]).astype(BF16)
     exchange(own_end, ends, send_b, recv_b)
     node_out[...] = result
+    lax.fori_loop(half, rows, pair_row, 0, unroll=2)
+    puts[1].start()
     own_out[...] = own_end[...].astype(F32)
     ends[mine, :] = own_end[...]
     settle(own_end, ends, send_b, recv_b)
     ends_out[...] = ends[...]
-    put_pre.wait()
+    puts[0].wait()
+    puts[1].wait()
 
 
 def edge_kernel(
@@ -483,7 +492,7 @@
             pltpu.VMEM((FRAME, FRAME), F32),
             pltpu.VMEM((4, WIDTH, d_node), BF16),
             pltpu.VMEM((lines, C_PAIR), F32),
-            pltpu.SemaphoreType.DMA((7,)),
+            pltpu.SemaphoreType.DMA((8,)),
             pltpu.SemaphoreType.DMA((n,)),
             pltpu.SemaphoreType.DMA((n,)),
             pltpu.SemaphoreType.DMA((n,)),

time: 30.2 us -> 30.2 us (level)
  no operation moved by 1% of the time
where the time goes in v5:
time: 30.2 us; the launch traced here: 30.1 us
  Pallas kernels  29.4 us (97%)
  between operations  0.64 us (2%)
    pallas_call x1, Pallas kernels, body(): pl.pallas_call(functools.partial(node_kernel, n), out_shape=(jax.ShapeDty...  21.4 us
    pallas_call x1, Pallas kernels, body(): pl.pallas_call(functools.partial(edge_kernel, step_rows), out_shape=(jax....  8.02 us

profile of v5, /device:TPU:0, one launch (start us, length us, event | category | flops | bytes accessed | tf_op | source)
XLA Modules:
  0.0 30.1 jit_solution(9250315690654408563)
XLA Ops:
  0.6 21.4 %node.1 = (bf16[16,256]{1,0:T(8,128)(2,1)}, bf16[256,128]{1,0:T(8,128)(2,1)}, f32[16,128]{1,0:T(8,128)}, bf16[16,256,384]{2,1,0:T(8,128)(2,1)}) custom-call(bf16[16,256]{1,0:T(8,128)(2,1)} %node_feats.1, bf16[3,16]{1,0:T(4,128)(2,1)} %bitcast.17, s32[3,16]{1,0:T(4,128)} %bitcast.16, s32[1,256]{1,0:T(1,128)} %bitcast.14, s32[1,256]{1,0:T(1,128)} %bitcast.18, ...), custom_call_target="tpu_custom_call" | custom-call | tf_op jit(solution)/shard_map/node/pallas_call | solution.py:469
  22.0 8.0 %edge.1 = (bf16[16,256]{1,0:T(8,128)(2,1)}, bf16[16,256,128]{2,1,0:T(8,128)(2,1)}) custom-call(bf16[16,256,128]{2,1,0:T(8,128)(2,1)} %pair.1, bf16[16,256,384]{2,1,0:T(8,128)(2,1)} %get-tuple-element.6.pre0, bf16[256,128]{1,0:T(8,128)(2,1)} %get-tuple-element.7.ends, f32[16,128]{1,0:T(8,128)} %get-tuple-element.8.own, ...), custom_call_target="tpu_custom_call" | custom-call | tf_op jit(solution)/shard_map/edge/pallas_call | solution.py:542
